TPU v7x, 512 devices: a whole 4x8x8 slice. The times are simulated.
512 devices in a mesh: site: 16 (over z, core), col: 32 (over x, y).
Axes of the slice: x: 4, y: 8, z: 8, core: 2. Of those that a mesh axis runs over, the one named last changes fastest.
Arguments:
- state_prev: float32 [128, 128, 8192], P('site', None, 'col'), may hold values from -6 to 6
- state_cur: float32 [128, 128, 8192], P('site', None, 'col'), may hold values from -6 to 6
- occupancy: int32 [4, 128, 128], replicated, may hold values 0 or 1
- panel_order: int32 [32], replicated, may hold values from 0 to 31, each once
Outputs:
- ortho_states: float32 [128, 128, 8192], P('site', None, 'col')
- growth: float32 [2, 256], replicated
Inputs may be any that keep to these rules, and one draw needn't show every extreme that they name: panel_order holds each panel number once.
All inputs are finite; a program needn't handle non-finite values.
Results may differ from a plain program's by a relative error of at most 0.000075.
Values sent between devices are 32-bit elements; how exact they have to be, the bound alone decides.
No kernel may reach another device: no remote copies, remote signals or barrier semaphores. Data moves between devices by JAX's collectives and lax.ppermute only.
A program may use at most 64 MiB of HBM per device.

v0:
```python
import jax
import jax.numpy as jnp
from jax import lax
from jax.sharding import PartitionSpec as P

STEPS = 4
PANEL = 256
ENERGY = 0.5
RESCALE = 0.015625


def from_root(value, axis, root):
    mine = lax.axis_index(axis) == root
    return lax.psum(jnp.where(mine, value, jnp.zeros_like(value)), axis)


def padded_2(value, sides, width):
    for axis, dim in sides:
        size, length = (lax.axis_size(axis), value.shape[dim])
        up = [(i, (i + 1) % size) for i in range(size)]
        down = [(j, i) for i, j in up]
        last = lax.slice_in_dim(value, length - width, length, axis=dim)
        leading = lax.slice_in_dim(value, 0, width, axis=dim)
        before = lax.ppermute(last, axis, up)
        after = lax.ppermute(leading, axis, down)
        value = jnp.concatenate([before, value, after], axis=dim)
    return value


def product(left, right):
    return jnp.dot(left, right, precision=lax.Precision.HIGHEST, preferred_element_type=jnp.float32)


def fetch_panel(flat, panel):
    count = PANEL // flat.shape[1]
    pieces = from_root(flat, "col", panel * count + 0)
    return pieces


def apply_inverse(lower, block):
    return jax.scipy.linalg.solve_triangular(lower, block.T, lower=True).T


def sweep_panel(flat, panel):
    block = fetch_panel(flat, panel)
    lower = jnp.linalg.cholesky(lax.psum(product(block.T, block), "site"))
    ortho = apply_inverse(lower, block)
    flat = flat - product(ortho, lax.psum(product(ortho.T, flat), "site"))
    return (flat, lower, ortho)


def place(result, ortho, panel, side):
    width = result.shape[1]
    offset = (lax.axis_index("col") - panel * (PANEL // width)) * width
    inside = jnp.logical_and(offset >= 0, offset < PANEL)
    return jnp.where(inside, ortho * float(side), result)


def on_device(state_prev, state_cur, occupancy, panel_order):
    rows, side, width = state_cur.shape
    start = lax.axis_index("site") * rows
    local_mask = lax.dynamic_slice_in_dim(occupancy, start, rows, 1)
    previous, current = (state_prev, state_cur)
    for turn in range(STEPS):
        weights = local_mask[turn].astype(jnp.float32)[:, :, None]
        padded = padded_2(current, (("site", 0),), 1)
        neighbours = padded[2:] + padded[:-2] + jnp.roll(current, 1, 1) + jnp.roll(current, -1, 1)
        previous, current = (current, weights * (ENERGY * current - neighbours - previous))
    flat = current.reshape(rows * side, width)
    first_panel = panel_order[0]
    second_panel = panel_order[1]
    flat, first_lower, first_q = sweep_panel(flat, first_panel)
    flat, second_lower, second_q = sweep_panel(flat, second_panel)
    result = flat * RESCALE
    result = place(result, first_q, first_panel, side)
    result = place(result, second_q, second_panel, side)
    growth = jnp.stack([jnp.log(jnp.diagonal(first_lower)), jnp.log(jnp.diagonal(second_lower))])
    return (result.reshape(rows, side, width), growth)


def solution(mesh):
    return jax.shard_map(
        on_device,
        mesh=mesh,
        in_specs=(P("site", None, "col"), P("site", None, "col"), P(), P()),
        out_specs=(P("site", None, "col"), P()),
        check_vma=False,
    )
```

profile of v0, /device:TPU:1, one launch (start us, length us, event | category | flops | bytes accessed | tf_op | source)
XLA Modules:
  0.0 974.7 jit_solution(11955733928134964861)
XLA Ops:
  7.2 1.0 fusion.76
  8.2 6.9 collective-permute-start
  15.1 0.9 fusion.75
  16.0 2.8 fusion.74
  20.0 0.7 fusion.56
  20.8 1.9 fusion.26
  22.9 3.1 collective-permute-start.2
  26.1 1.3 collective-permute-done.2
  27.3 2.5 collective-permute-done.3
  30.5 4.8 collective-permute-start.4
  35.3 1.0 collective-permute-done.4
  36.2 1.0 collective-permute-done.5
  37.8 3.7 collective-permute-start.6
  41.5 1.4 collective-permute-done.6
  44.9 1.1 broadcast_select_fusion.1
  46.1 155.3 %all-reduce.8.cloned.1.call-done = f32[1024,256]{0,1:T(8,128)} async-done(((f32[1024,256]{0,1:T(8,128)}), f32[1024,256]{0,1:T(8,128)}) %all-reduce.8.cloned.1.call-update) | async-done | bytes 1048592 | tf_op jit(solution)/shard_map/psum | solution.py:14
  201.3 3.3 fusion.78
  205.0 116.8 %all-reduce.10.cloned.1.call-done = f32[256,256]{0,1:T(8,128)} async-done(((f32[256,256]{0,1:T(8,128)}), f32[256,256]{0,1:T(8,128)}) %all-reduce.10.cloned.1.call-update) | async-done | bytes 262160 | tf_op jit(solution)/shard_map/psum | solution.py:46
  321.7 1.1 copy.16
  323.0 11.7 %cholesky.130 = f32[128,128]{1,0:T(8,128)S(1)} custom-call(f32[128,128]{1,0:T(8,128)S(1)} %cholesky.194), custom_call_target="Cholesky" | custom-call | tf_op jit(solution)/shard_map/jit(cholesky)/cholesky | solution.py:46
  334.7 9.8 %custom-call.17 = f32[1,128,128]{1,2,0:T(8,128)S(1)} custom-call(f32[1,128,128]{2,1,0:T(8,128)S(1)} %get-tuple-element.83), custom_call_target="InvertDiagBlocksLowerTriangular" | custom-call | tf_op jit(solution)/shard_map/jit(cholesky)/cholesky | solution.py:46
  345.0 11.7 %cholesky.147 = f32[128,128]{1,0:T(8,128)S(1)} custom-call(f32[128,128]{1,0:T(8,128)S(1)} %convolution_subtract_fusion.5), custom_call_target="Cholesky" | custom-call | tf_op jit(solution)/shard_map/jit(cholesky)/cholesky | solution.py:46
  358.9 4.6 while.4
  360.1 1.3 bitcast_dynamic-update-slice_fusion.4
  362.1 1.3 bitcast_dynamic-update-slice_fusion.4
  363.5 19.7 %custom-call.18 = f32[2,128,128]{1,2,0:T(8,128)S(1)} custom-call(f32[2,128,128]{2,1,0:T(8,128)S(1)} %get-tuple-element.18), custom_call_target="InvertDiagBlocksLowerTriangular" | custom-call | tf_op jit(solution)/shard_map/jit(_solve_triangular)/triangular_solve | solution.py:41
  385.1 1.7 fusion.28
  387.5 113.8 %all-reduce.12.cloned.1.call-done = f32[256,256]{1,0:T(8,128)} async-done(((f32[256,256]{1,0:T(8,128)}), f32[256,256]{1,0:T(8,128)}) %all-reduce.12.cloned.1.call-update) | async-done | bytes 262160 | tf_op jit(solution)/shard_map/psum | solution.py:48
  501.3 3.4 broadcast_select_fusion
  504.7 156.2 %all-reduce.14.cloned.1.call-done = f32[1024,256]{0,1:T(8,128)} async-done(((f32[1024,256]{0,1:T(8,128)}), f32[1024,256]{0,1:T(8,128)}) %all-reduce.14.cloned.1.call-update) | async-done | bytes 1048592 | tf_op jit(solution)/shard_map/psum | solution.py:14
  660.9 3.3 fusion.79
  664.4 116.7 %all-reduce.16.cloned.1.call-done = f32[256,256]{0,1:T(8,128)} async-done(((f32[256,256]{0,1:T(8,128)}), f32[256,256]{0,1:T(8,128)}) %all-reduce.16.cloned.1.call-update) | async-done | bytes 262160 | tf_op jit(solution)/shard_map/psum | solution.py:46
  781.1 1.1 copy.19
  782.4 11.7 %cholesky.164 = f32[128,128]{1,0:T(8,128)S(1)} custom-call(f32[128,128]{1,0:T(8,128)S(1)} %cholesky.197), custom_call_target="Cholesky" | custom-call | tf_op jit(solution)/shard_map/jit(cholesky)/cholesky | solution.py:46
  794.8 9.8 %custom-call.19 = f32[1,128,128]{1,2,0:T(8,128)S(1)} custom-call(f32[1,128,128]{2,1,0:T(8,128)S(1)} %get-tuple-element.79), custom_call_target="InvertDiagBlocksLowerTriangular" | custom-call | tf_op jit(solution)/shard_map/jit(cholesky)/cholesky | solution.py:46
  805.1 11.7 %cholesky.181 = f32[128,128]{1,0:T(8,128)S(1)} custom-call(f32[128,128]{1,0:T(8,128)S(1)} %convolution_subtract_fusion.4), custom_call_target="Cholesky" | custom-call | tf_op jit(solution)/shard_map/jit(cholesky)/cholesky | solution.py:46
  816.8 0.7 compare_reduce_fusion
  818.9 0.7 fusion.38
  819.6 4.1 while.5
  820.5 1.3 bitcast_dynamic-update-slice_fusion.5
  822.4 1.3 bitcast_dynamic-update-slice_fusion.5
  823.7 19.7 %custom-call.20 = f32[2,128,128]{1,2,0:T(8,128)S(1)} custom-call(f32[2,128,128]{2,1,0:T(8,128)S(1)} %get-tuple-element.19), custom_call_target="InvertDiagBlocksLowerTriangular" | custom-call | tf_op jit(solution)/shard_map/jit(_solve_triangular)/triangular_solve | solution.py:41
  845.3 1.7 fusion.27
  848.3 2.3 gather_fusion
  850.7 2.3 gather_fusion.1
  853.7 107.9 %all-reduce.18.cloned.1.call-done = f32[256,256]{1,0:T(8,128)} async-done(((f32[256,256]{1,0:T(8,128)}), f32[256,256]{1,0:T(8,128)}) %all-reduce.18.cloned.1.call-update) | async-done | bytes 262160 | tf_op jit(solution)/shard_map/psum | solution.py:48
  961.5 3.6 fusion.2
  965.1 2.5 copy.27
  (96 shorter events, 14.4 us)
Async XLA Ops:
  7.2 194.2 %all-reduce.8.cloned.1.call-start = ((), (), s32[]{:S(2)}) async-start(), calls=%async_computation | async-start | bytes 2097152 | tf_op jit(solution)/shard_map/psum | solution.py:14
  8.2 12.5 %collective-permute-start = (f32[1,128,256]{2,1,0:T(8,128)S(1)}, f32[1,128,256]{2,1,0:T(8,128)S(1)}, u32[]{:S(2)}, u32[]{:S(2)}) collective-permute-start(f32[1,128,256]{2,1,0:T(8,128)S(1)} %get-tuple-element.70), channel_id=1, source_target_pairs={{32,0},{64,32},{96,64},{128,96},{160,128},{192,160},{224,192},{256... | collective-permute-start | bytes 393224 | tf_op jit(solution)/shard_map/ppermute | solution.py:25
  15.1 5.7 collective-permute-start.1
  16.0 2.8 copy-start.11
  16.0 4.8 copy-start
  22.9 4.4 collective-permute-start.2
  26.0 3.8 collective-permute-start.3
  30.5 5.8 collective-permute-start.4
  35.3 2.0 collective-permute-start.5
  37.8 5.1 collective-permute-start.6
  41.5 2.0 collective-permute-start.7
  43.9 1.0 copy-start.5
  46.0 275.7 %all-reduce.10.cloned.1.call-start = ((), (), s32[]{:S(2)}) async-start(), calls=%async_computation.1 | async-start | bytes 524288 | tf_op jit(solution)/shard_map/psum | solution.py:46
  204.6 296.7 %all-reduce.12.cloned.1.call-start = ((), (), s32[]{:S(2)}) async-start(), calls=%async_computation.2 | async-start | bytes 524288 | tf_op jit(solution)/shard_map/psum | solution.py:48
  321.7 1.2 copy-start.9
  344.8 38.4 %copy-start.1 = (f32[1024,256]{0,1:T(8,128)S(1)}, f32[1024,256]{0,1:T(8,128)}, u32[]{:S(2)}) copy-start(f32[1024,256]{0,1:T(8,128)} %all-reduce.8.cloned.1.call-done) | copy-start | bytes 3145732
  383.8 1.2 copy-start.6
  386.8 274.1 %all-reduce.14.cloned.1.call-start = ((), (), s32[]{:S(2)}) async-start(), calls=%async_computation.3 | async-start | bytes 2097152 | tf_op jit(solution)/shard_map/psum | solution.py:14
  504.7 276.4 %all-reduce.16.cloned.1.call-start = ((), (), s32[]{:S(2)}) async-start(), calls=%async_computation.4 | async-start | bytes 524288 | tf_op jit(solution)/shard_map/psum | solution.py:46
  664.2 297.3 %all-reduce.18.cloned.1.call-start = ((), (), s32[]{:S(2)}) async-start(), calls=%async_computation.5 | async-start | bytes 524288 | tf_op jit(solution)/shard_map/psum | solution.py:48
  781.1 1.2 copy-start.10
  804.8 38.6 %copy-start.2 = (f32[1024,256]{0,1:T(8,128)S(1)}, f32[1024,256]{0,1:T(8,128)}, u32[]{:S(2)}) copy-start(f32[1024,256]{0,1:T(8,128)} %all-reduce.14.cloned.1.call-done) | copy-start | bytes 3145732
  844.1 1.3 copy-start.3
  845.3 1.8 copy-start.7
  848.3 2.4 copy-start.8
  848.3 113.2 %copy-start.4 = (f32[1024,256]{0,1:T(8,128)S(1)}, f32[1024,256]{0,1:T(8,128)}, u32[]{:S(2)}) copy-start(f32[1024,256]{0,1:T(8,128)} %get-tuple-element.89) | copy-start | bytes 3145732
Sparse Core Ops, SparseCore 0:
  46.1 155.1 all-reduce.7
  204.7 116.9 all-reduce.9
  386.9 114.3 all-reduce.11
  505.1 155.7 all-reduce.13
  664.3 116.7 all-reduce.15
  847.2 114.2 all-reduce.17
where the time goes:
time: 979 us; the launch traced here: 975 us
  waiting for transfers between devices  774 us (79%)
  other arithmetic  115 us (12%)
  local copies, waits for them, and re-layouts  24.4 us (2%)
  matrix products  21.6 us (2%)
  between operations  19.9 us (2%)
  starting transfers between devices  19.2 us (2%)
    psum x2, waiting for transfers between devices, from_root(): return lax.psum(jnp.where(mine, value, jnp.zeros_like(value)), axis)  311 us
    psum x2, waiting for transfers between devices, sweep_panel(): lower = jnp.linalg.cholesky(lax.psum(product(block.T, block), 'site'))  233 us
    psum x2, waiting for transfers between devices, sweep_panel(): flat = flat - product(ortho, lax.psum(product(ortho.T, flat), 'site'))  222 us
    another operation x13, other arithmetic, sweep_panel(): lower = jnp.linalg.cholesky(lax.psum(product(block.T, block), 'site'))  68.7 us
    another operation x5, other arithmetic, apply_inverse(): return jax.scipy.linalg.solve_triangular(lower, block.T, lower=True).T  40.1 us
  transfers between devices with their start and end apart: 14, of which 12 were waited for; matrix products, arithmetic and copies ran while one was open for 1% of the time, Pallas kernels for 0%

commit v1 on v0

--- a/solution.py
+++ b/solution.py
@@ -9,9 +9,14 @@
 RESCALE = 0.015625
 
 
+def _lead_local_data(packet, which_axis):
+    then = lax.all_gather(packet, axis_name=which_axis)
+    return jnp.sum(then, axis=0)
+
+
 def from_root(value, axis, root):
     mine = lax.axis_index(axis) == root
-    return lax.psum(jnp.where(mine, value, jnp.zeros_like(value)), axis)
+    return _lead_local_data(jnp.where(mine, value, jnp.zeros_like(value)), axis)
 
 
 def padded_2(value, sides, width):

time: 979 us -> 1190 us (1.22)
  waiting for transfers between devices: 774 us -> 928 us
  local copies, waits for them, and re-layouts: 24.4 us -> 54.1 us
  other arithmetic: 115 us -> 138 us
    all_gather x0 -> x2, waiting for transfers between devices: none -> 475 us  [_lead_local_data(): then = lax.all_gather(packet, axis_name=which_axis)]
    psum x2 -> x0, waiting for transfers between devices: 311 us -> none  [from_root(): return lax.psum(jnp.where(mine, value, jnp.zeros_like(value)), axis)]
    unnamed x25 -> x8, local copies, waits for them, and re-layouts: 3.21 us -> 32 us
    reduce_sum x0 -> x2, other arithmetic: none -> 19.4 us  [_lead_local_data(): return jnp.sum(then, axis=0)]
where the time goes in v1:
time: 1190 us; the launch traced here: 1180 us
  waiting for transfers between devices  928 us (78%)
  other arithmetic  138 us (12%)
  local copies, waits for them, and re-layouts  54.1 us (5%)
  matrix products  23.4 us (2%)
  starting transfers between devices  19.7 us (2%)
  between operations  19.7 us (2%)
    all_gather x2, waiting for transfers between devices, _lead_local_data(): then = lax.all_gather(packet, axis_name=which_axis)  475 us
    psum x2, waiting for transfers between devices, sweep_panel(): lower = jnp.linalg.cholesky(lax.psum(product(block.T, block), 'site'))  224 us
    psum x2, waiting for transfers between devices, sweep_panel(): flat = flat - product(ortho, lax.psum(product(ortho.T, flat), 'site'))  221 us
    another operation x13, other arithmetic, sweep_panel(): lower = jnp.linalg.cholesky(lax.psum(product(block.T, block), 'site'))  68.6 us
    another operation x5, other arithmetic, apply_inverse(): return jax.scipy.linalg.solve_triangular(lower, block.T, lower=True).T  40.1 us
    unnamed x8, local copies, waits for them, and re-layouts  32 us
  transfers between devices with their start and end apart: 14, of which 12 were waited for; matrix products, arithmetic and copies ran while one was open for 1% of the time, Pallas kernels for 0%

profile of v1, /device:TPU:1, one launch (start us, length us, event | category | flops | bytes accessed | tf_op | source)
XLA Modules:
  0.0 1182.4 jit_solution(5662960657726558692)
XLA Ops:
  8.2 6.9 collective-permute-start
  16.0 1.8 fusion.75
  17.8 1.3 fusion.78
  20.5 2.6 fusion.26
  23.3 3.3 collective-permute-start.2
  27.7 2.5 collective-permute-done.3
  30.2 1.7 fusion.20
  32.1 4.8 collective-permute-start.4
  39.5 3.7 collective-permute-start.6
  43.2 1.4 collective-permute-done.6
  45.2 1.4 broadcast_select_fusion.1
  46.6 237.2 %all-gather.4.cloned.1.call-done = f32[32,1024,256]{2,1,0:T(8,128)} async-done(((f32[1,1024,256]{2,1,0:T(8,128)}), f32[32,1024,256]{2,1,0:T(8,128)}) %all-gather.4.cloned.1.call-update) | async-done | bytes 33554448 | tf_op jit(solution)/shard_map/all_gather | solution.py:13
  283.8 11.9 %reduce_sum.18 = f32[1024,256]{1,0:T(8,128)S(1)} reduce(f32[32,1024,256]{2,1,0:T(8,128)} %all-gather.4.cloned.1.call-done, f32[]{:T(128)} %constant.88.clone.1), dimensions={0}, to_apply=%region_0.1 | reduce | flops 8126464 | bytes 34603012 | tf_op jit(solution)/shard_map/reduce_sum | solution.py:14
  295.7 2.5 fusion.79
  298.9 1.3 copy.33
  300.2 110.9 %all-reduce.6.cloned.1.call-done = f32[256,256]{0,1:T(8,128)} async-done(((f32[256,256]{0,1:T(8,128)}), f32[256,256]{0,1:T(8,128)}) %all-reduce.6.cloned.1.call-update) | async-done | bytes 262160 | tf_op jit(solution)/shard_map/psum | solution.py:51
  413.2 11.7 cholesky.130
  425.0 9.8 custom-call.17
  435.3 11.7 cholesky.147
  449.0 4.0 while.4
  449.8 1.3 bitcast_dynamic-update-slice_fusion.4
  451.7 1.3 bitcast_dynamic-update-slice_fusion.4
  453.0 19.7 %custom-call.18 = f32[2,128,128]{1,2,0:T(8,128)S(1)} custom-call(f32[2,128,128]{2,1,0:T(8,128)S(1)} %get-tuple-element.18), custom_call_target="InvertDiagBlocksLowerTriangular" | custom-call | tf_op jit(solution)/shard_map/jit(_solve_triangular)/triangular_solve | solution.py:46
  472.7 1.7 fusion.31
  474.4 1.6 convolution_subtract_fusion.3
  476.7 1.7 fusion.28
  479.4 113.4 %all-reduce.8.cloned.1.call-done = f32[256,256]{1,0:T(8,128)} async-done(((f32[256,256]{1,0:T(8,128)}), f32[256,256]{1,0:T(8,128)}) %all-reduce.8.cloned.1.call-update) | async-done | bytes 262160 | tf_op jit(solution)/shard_map/psum | solution.py:53
  592.9 3.0 broadcast_select_fusion
  596.0 238.1 %all-gather.6.cloned.1.call-done = f32[32768,256]{0,1:T(8,128)} async-done(((f32[1024,256]{0,1:T(8,128)}), f32[32768,256]{0,1:T(8,128)}) %all-gather.6.cloned.1.call-update) | async-done | bytes 33554448 | tf_op jit(solution)/shard_map/all_gather | solution.py:13
  834.1 28.8 %copy.45 = f32[32,8,32,1024]{3,2,1,0:T(8,128)S(1)} copy(f32[32,8,32,1024]{3,1,2,0:T(8,128)} %bitcast.99) | data formatting | bytes 67108864
  862.9 7.5 bitcast_reduce_fusion
  870.4 1.7 fusion.80
  872.4 112.6 %all-reduce.10.cloned.1.call-done = f32[256,256]{0,1:T(8,128)} async-done(((f32[256,256]{0,1:T(8,128)}), f32[256,256]{0,1:T(8,128)}) %all-reduce.10.cloned.1.call-update) | async-done | bytes 262160 | tf_op jit(solution)/shard_map/psum | solution.py:51
  987.8 11.7 cholesky.164
  1000.2 9.8 custom-call.19
  1011.1 1.1 convolution_subtract_fusion.4
  1012.2 11.7 cholesky.181
  1026.7 4.1 while.5
  1027.5 1.3 bitcast_dynamic-update-slice_fusion.5
  1029.5 1.3 bitcast_dynamic-update-slice_fusion.5
  1030.7 19.7 %custom-call.20 = f32[2,128,128]{1,2,0:T(8,128)S(1)} custom-call(f32[2,128,128]{2,1,0:T(8,128)S(1)} %get-tuple-element.19), custom_call_target="InvertDiagBlocksLowerTriangular" | custom-call | tf_op jit(solution)/shard_map/jit(_solve_triangular)/triangular_solve | solution.py:46
  1051.1 1.4 convolution_subtract_fusion.2
  1053.1 1.7 fusion.27
  1056.2 2.3 gather_fusion
  1058.5 2.6 gather_fusion.1
  1061.7 107.7 %all-reduce.12.cloned.1.call-done = f32[256,256]{1,0:T(8,128)} async-done(((f32[256,256]{1,0:T(8,128)}), f32[256,256]{1,0:T(8,128)}) %all-reduce.12.cloned.1.call-update) | async-done | bytes 262160 | tf_op jit(solution)/shard_map/psum | solution.py:53
  1169.4 3.4 fusion.2
  1172.8 2.5 copy.44
  (81 shorter events, 23.0 us)
Async XLA Ops:
  7.2 276.7 %all-gather.4.cloned.1.call-start = ((), (), s32[]{:S(2)}) async-start(), calls=%async_computation | async-start | bytes 34603008 | tf_op jit(solution)/shard_map/all_gather | solution.py:13
  8.2 12.3 %collective-permute-start = (f32[1,128,256]{2,1,0:T(8,128)S(1)}, f32[1,128,256]{2,1,0:T(8,128)S(1)}, u32[]{:S(2)}, u32[]{:S(2)}) collective-permute-start(f32[1,128,256]{2,1,0:T(8,128)S(1)} %get-tuple-element.76), channel_id=1, source_target_pairs={{32,0},{64,32},{96,64},{128,96},{160,128},{192,160},{224,192},{256... | collective-permute-start | bytes 393224 | tf_op jit(solution)/shard_map/ppermute | solution.py:30
  15.1 5.4 collective-permute-start.1
  23.3 4.4 collective-permute-start.2
  26.6 3.6 collective-permute-start.3
  32.1 5.8 collective-permute-start.4
  36.9 2.0 collective-permute-start.5
  39.5 5.1 collective-permute-start.6
  43.2 2.0 collective-permute-start.7
  46.5 364.6 %all-reduce.6.cloned.1.call-start = ((), (), s32[]{:S(2)}) async-start(), calls=%async_computation.1 | async-start | bytes 524288 | tf_op jit(solution)/shard_map/psum | solution.py:51
  298.3 294.6 %all-reduce.8.cloned.1.call-start = ((), (), s32[]{:S(2)}) async-start(), calls=%async_computation.2 | async-start | bytes 524288 | tf_op jit(solution)/shard_map/psum | solution.py:53
  476.6 357.5 %copy-start = (f32[128,1024]{1,0:T(8,128)}, f32[128,1024]{1,0:T(8,128)S(1)}, u32[]{:S(2)}) copy-start(f32[128,1024]{1,0:T(8,128)S(1)} %fusion.44) | copy-start | bytes 1572868
  478.4 355.7 %all-gather.6.cloned.1.call-start = ((), (), s32[]{:S(2)}) async-start(), calls=%async_computation.5 | async-start | bytes 34603008 | tf_op jit(solution)/shard_map/all_gather | solution.py:13
  595.9 389.1 %all-reduce.10.cloned.1.call-start = ((), (), s32[]{:S(2)}) async-start(), calls=%async_computation.3 | async-start | bytes 524288 | tf_op jit(solution)/shard_map/psum | solution.py:51
  872.1 297.2 %all-reduce.12.cloned.1.call-start = ((), (), s32[]{:S(2)}) async-start(), calls=%async_computation.4 | async-start | bytes 524288 | tf_op jit(solution)/shard_map/psum | solution.py:53
  987.1 0.7 copy-start.2
  1030.7 19.7 %copy-start.1 = (f32[256,256]{1,0:T(8,128)}, f32[256,256]{1,0:T(8,128)S(1)}, u32[]{:S(2)}) copy-start(f32[256,256]{1,0:T(8,128)S(1)} %get-tuple-element.200) | copy-start | bytes 786436
Sparse Core Ops, SparseCore 0:
  46.7 237.0 all-gather.3
  298.4 112.6 all-reduce.5
  478.5 114.2 all-reduce.7
  596.5 237.6 all-gather.5
  872.3 112.7 all-reduce.9
  1055.0 114.3 all-reduce.11
